TPU v7x, 32 devices: a whole 2x2x4 slice. The times are simulated.
32 devices in a mesh: row: 8 (over z, y), col: 4 (over x, core).
Axes of the slice: x: 2, y: 2, z: 4, core: 2. Of those that a mesh axis runs over, the one named last changes fastest.
Arguments:
- momentum: float32 [8192, 16384], P('row', 'col'), may hold values from -6 to 6
- grads: bfloat16 [2, 8192, 16384], P(None, 'row', 'col'), may hold values from -400 to 400
- basis: float32 [16384, 256], P('col'), may hold values from -0.046875 to 0.046875
Outputs:
- change: bfloat16 [8192, 16384], P('row', 'col')
- state: float32 [8192, 16384], P('row', 'col')
All inputs are finite; a program needn't handle non-finite values.
Results may differ from a plain program's by a relative error of at most 0.0035.
Values sent between devices are 32-bit elements; how exact they have to be, the bound alone decides.
A program may use at most 192 MiB of HBM per device.

v0:
```python
import functools

import jax
import jax.numpy as jnp
from jax import lax
from jax.experimental import pallas as pl
from jax.experimental.pallas import tpu as pltpu
from jax.sharding import PartitionSpec as P

keep_rate = 0.95
norm_eps = 1e-06
HIGH = lax.Precision.HIGH
HIGHEST = lax.Precision.HIGHEST
MESH = pl.DeviceIdType.MESH
LANES = 128
STRIDE = 2
SLOTS = 3
WIDTH = 256


def matmul(a, b, dims, precision):
    return lax.dot_general(a, b, (dims, ((), ())), precision=precision, preferred_element_type=jnp.float32)


def split(x):
    high = x.astype(jnp.bfloat16)
    return high, (x - high.astype(jnp.float32)).astype(jnp.bfloat16)


KINDS = 12


def row_kernel(rows, cols, step, *refs):
    state, refs = refs[0], refs[1:]
    if step is not None:
        grads, refs = refs[0], refs[1:]
    projected, ortho, raw, scale, refs = *refs[:4], refs[4:]
    fin, work, upward, pair, turned, factor, panel, squares, slots, states, refs = *refs[:10], refs[10:]
    if step is not None:
        slopes, refs = refs[0], refs[1:]
    load_sem, send_sem, recv_sem, norm_send, norm_recv = refs
    line = rows // 2
    rank = factor.shape[0]
    first = rank // WIDTH
    chunks = fin.shape[0]
    size = rank // 8
    me = lax.axis_index("row")
    y = lax.rem(me, 2)
    z = me // 2
    partner = me + 1 - 2 * y
    mine = pl.multiple_of(2 * size * y, 8)
    yours = pl.multiple_of(2 * size * (1 - y), 8)
    away = (z, line - 1 - z)
    nearer = (me - 2, me + 2)
    farther = (me + 2, me - 2)
    one = tuple(pl.multiple_of(mine + size * p, 8) for p in range(2))
    two = tuple(4 * size + 2 * size * p for p in range(2))

    def load(j, slot):
        columns = pl.ds(pl.multiple_of(j * WIDTH, WIDTH), WIDTH)
        copies = [pltpu.make_async_copy(state.at[:, columns], states.at[slot], load_sem.at[0, slot])]
        if step is not None:
            copies.append(pltpu.make_async_copy(grads.at[step, :, columns], slopes.at[slot], load_sem.at[1, slot]))
        return copies

    for j in range(SLOTS - 1):
        for copy in load(j, j):
            copy.start()

    def send(kind, c, source, start, target, at, count, device):
        return pltpu.make_async_remote_copy(
            src_ref=source.at[c, pl.ds(start, count)],
            dst_ref=target.at[c, pl.ds(at, count)],
            send_sem=send_sem.at[kind, c],
            recv_sem=recv_sem.at[kind, c],
            device_id={"row": device},
            device_id_type=MESH,
        )

    copies = {0: lambda c: send(0, c, work, yours, pair, 0, 2 * size, partner)}
    for p in range(2):
        n, f, o, t = nearer[p], farther[p], one[p], two[p]
        up = upward.at[p]
        copies[1 + p] = functools.partial(send, 1 + p, source=work, start=o, target=up, at=0, count=size, device=n)
        copies[3 + p] = functools.partial(
            send, 3 + p, source=work, start=t, target=up, at=size, count=2 * size, device=n
        )
        copies[6 + p] = functools.partial(send, 6 + p, source=fin, start=o, target=fin, at=o, count=size, device=f)
        copies[8 + p] = functools.partial(send, 8 + p, source=fin, start=t, target=fin, at=t, count=2 * size, device=f)
        copies[10 + p] = functools.partial(
            send, 10 + p, source=fin, start=o, target=fin, at=o, count=size, device=partner
        )
    cross = [
        functools.partial(
            send, 5, source=work, start=two[p], target=pair, at=2 * size, count=2 * size, device=partner
        )
        for p in range(2)
    ]

    def add(target, c, start, source, at, count):
        target[c, pl.ds(start, count), :] = work[c, pl.ds(start, count), :] + source[c, pl.ds(at, count), :]

    transposed = projected[...].T
    high, low = split(transposed)
    turned[0] = high
    turned[1] = low
    gram = matmul(transposed, transposed, ((1,), (1,)), HIGHEST)
    for k in range(first):
        work[k] = gram[:, k * WIDTH : (k + 1) * WIDTH]

    barrier = pltpu.get_barrier_semaphore()
    pl.semaphore_signal(barrier, inc=1, device_id={"row": partner}, device_id_type=MESH)
    for p in range(2):
        @pl.when(away[p] > 0)
        def _():
            pl.semaphore_signal(barrier, inc=1, device_id={"row": nearer[p]}, device_id_type=MESH)

    mine_col = lax.axis_index("col")
    others = [lax.rem(mine_col + d, cols) for d in range(1, cols)]
    for other in others:
        pl.semaphore_signal(barrier, inc=1, device_id={"col": other}, device_id_type=MESH)
    pl.semaphore_wait(barrier, jnp.where((z == 0) | (z == line - 1), 2, 3) + cols - 1)

    turn = line * STRIDE
    delay = max(turn, chunks + 1 - 2 * STRIDE) - turn
    last = 2 * turn + delay

    block = 32
    per = 16
    pieces = rank // per
    begin = 2 * turn + first

    def eliminate(t):
        k0 = (t * per // block) * block
        part = t % (block // per)
        tile = (k0 // LANES) * LANES
        shift = k0 % LANES
        r = lax.broadcasted_iota(jnp.int32, (block, LANES), 0)
        l = lax.broadcasted_iota(jnp.int32, (block, LANES), 1)
        if part == 0:
            d = factor[k0 : k0 + block, tile : tile + LANES]
            if shift:
                d = pltpu.roll(d, LANES - shift, 1)
            aug = jnp.where(l < block, d, jnp.where(l - block == r, 1.0, 0.0))
        else:
            aug = panel[...]
        for j in range(part * per, (part + 1) * per):
            column = jnp.broadcast_to(aug[:, j : j + 1], (block, LANES))
            pivot = column[j : j + 1, :]
            ratio = jnp.where(r > j, column * (1.0 / pivot), 0.0)
            aug = aug - ratio * aug[j : j + 1, :]
        if part < block // per - 1:
            panel[...] = aug
            return
        diagonal = jnp.sum(jnp.where(l == r, aug, 0.0), axis=1, keepdims=True)
        t_inv = (aug * lax.rsqrt(diagonal))[:, block : 2 * block]
        rw = lax.broadcasted_iota(jnp.int32, (block, rank), 0)
        lw = lax.broadcasted_iota(jnp.int32, (block, rank), 1)
        inside = (lw >= k0) & (lw < k0 + block)
        own = jnp.where(inside, jnp.where(lw - k0 == rw, 1.0, 0.0), factor[k0 : k0 + block, :])
        done = matmul(t_inv, own, ((1,), (0,)), HIGHEST)
        factor[k0 : k0 + block, :] = done
        rest = rank - k0 - block
        if rest:
            below = factor[k0 + block :, :]
            left_part = matmul(below[:, k0 : k0 + block], t_inv, ((1,), (1,)), HIGHEST)
            lb = lax.broadcasted_iota(jnp.int32, (rest, rank), 1)
            kept = jnp.where((lb >= k0) & (lb < k0 + block), 0.0, below)
            factor[k0 + block :, :] = kept - matmul(left_part, done, ((1,), (0,)), HIGHEST)

    def finish():
        r = lax.broadcasted_iota(jnp.int32, (rank, rank), 0)
        l = lax.broadcasted_iota(jnp.int32, (rank, rank), 1)
        inverse = jnp.where(l <= r, factor[...], 0.0)
        high, low = split(inverse)
        turned[0, :, :rank] = high
        turned[1, :, :rank] = low
        ortho[...] = matmul(projected[...], inverse, ((1,), (1,)), HIGHEST)
        squares[...] = jnp.zeros_like(squares)

    def expand(c):
        t_high, t_low = split(fin[c])
        i_high, i_low = turned[0, :, :rank], turned[1, :, :rank]
        dims = ((1,), (0,))
        value = matmul(i_high, t_high, dims, None) + matmul(i_high, t_low, dims, None) + matmul(i_low, t_high, dims, None)
        raw[c - first] = value
        square = value * value
        squares[...] += sum(square[:, k : k + LANES] for k in range(0, WIDTH, LANES))

    total = chunks + last
    ready = max(begin + pieces, chunks)

    def reached(i):
        count = jnp.minimum(jnp.minimum(first + 3 * (i - ready + 1), i - (last - 1) + 1), chunks)
        return jnp.maximum(count, first)

    @pl.loop(0, total)
    def _(i):
        @pl.when(i < chunks)
        def _():
            c = i

            @pl.when(c >= first)
            def _():
                j = c - first
                slot = lax.rem(j, SLOTS)
                ahead = j + SLOTS - 1

                @pl.when(ahead < chunks - first)
                def _():
                    for copy in load(ahead, lax.rem(ahead, SLOTS)):
                        copy.start()

                for copy in load(j, slot):
                    copy.wait()
                buffer = states[slot]
                if step is not None:
                    buffer = buffer + slopes[slot].astype(jnp.float32)
                b_high, b_low = split(buffer)
                dims = ((1,), (0,))
                work[c] = (
                    matmul(turned[0], b_high, dims, None)
                    + matmul(turned[0], b_low, dims, None)
                    + matmul(turned[1], b_high, dims, None)
                )

            copies[0](c).start()

        def stage(offset, action, when=True, low=0, high=chunks):
            c = i - offset

            @pl.when((c >= low) & (c < high) & when)
            def _():
                action(c)

        def paired(c):
            copies[0](c).wait_recv()
            add(work, c, mine, pair, 0, 2 * size)

        def rise_one(c, p):
            @pl.when(away[p] < line - 1)
            def _():
                copies[1 + p](c).wait_recv()

                @pl.when(away[p] > 0)
                def _():
                    add(work, c, one[p], upward.at[p], 0, size)

                @pl.when(away[p] == 0)
                def _():
                    add(fin, c, one[p], upward.at[p], 0, size)

            @pl.when(away[p] > 0)
            def _():
                copies[1 + p](c).start()

        def rise_two(c, p):
            @pl.when(away[p] < line - 1)
            def _():
                copies[3 + p](c).wait_recv()
                add(work, c, two[p], upward.at[p], size, 2 * size)

            @pl.when(away[p] > 0)
            def _():
                copies[3 + p](c).start()

        def exchange(c, p):
            cross[p](c).start()

        def crossed(c, p):
            cross[p](c).wait_recv()
            add(fin, c, two[p], pair, 2 * size, 2 * size)

        def fall(c, p):
            @pl.when(away[p] > 0)
            def _():
                copies[6 + p](c).wait_recv()

            @pl.when(away[p] < line - 1)
            def _():
                copies[6 + p](c).start()

            copies[10 + p](c).start()

            @pl.when(away[p] > 0)
            def _():
                copies[8 + p](c).wait_recv()

            @pl.when(away[p] < line - 1)
            def _():
                copies[8 + p](c).start()

        def gathered(c):
            copies[10](c).wait_recv()
            copies[11](c).wait_recv()

        stage(STRIDE, paired)
        for p in range(2):
            height = (line - 1 - away[p]) * STRIDE
            stage(height, functools.partial(rise_two, p=p))
            stage(STRIDE + height, functools.partial(rise_one, p=p))
        for low, high, later in ((0, first, 0), (first, chunks, delay)):
            for p in range(2):
                at = turn - STRIDE + later // 2
                stage(at, functools.partial(exchange, p=p), away[p] == 0, low, high)
                stage(at + STRIDE, functools.partial(crossed, p=p), away[p] == 0, low, high)
                stage(turn + later + away[p] * STRIDE, functools.partial(fall, p=p), True, low, high)
            stage(2 * turn + later - 1, gathered, True, low, high)

        for t in range(pieces):
            @pl.when(i == begin + t)
            def _():
                if t == 0:
                    gram = jnp.concatenate([fin[k] for k in range(first)], axis=1)
                    factor[...] = 0.5 * (gram + gram.T)
                eliminate(t)

        if ready < total:
            @pl.when(i == ready)
            def _():
                finish()

            @pl.when(i >= ready)
            def _():
                @pl.loop(reached(i - 1), reached(i))
                def _(c):
                    expand(c)

    for t in range(pieces):
        if total <= begin + t:
            if t == 0:
                gram = jnp.concatenate([fin[k] for k in range(first)], axis=1)
                factor[...] = 0.5 * (gram + gram.T)
            eliminate(t)
    if total <= ready:
        finish()

    done = min(max(first + 3 * (total - ready), first), chunks) if ready < total else first

    @pl.loop(done, chunks)
    def _(c):
        expand(c)

    slots[mine_col] = matmul(jnp.ones((8, LANES), jnp.float32), squares[...], ((1,), (1,)), HIGHEST)
    norms = [
        pltpu.make_async_remote_copy(
            src_ref=slots.at[mine_col],
            dst_ref=slots.at[mine_col],
            send_sem=norm_send.at[d],
            recv_sem=norm_recv.at[d],
            device_id={"col": other},
            device_id_type=MESH,
        )
        for d, other in enumerate(others)
    ]
    for copy in norms:
        copy.start()

    @pl.loop(0, chunks)
    def _(c):
        for kind in (0, 10, 11):
            copies[kind](c).wait_send()
        for p in range(2):
            @pl.when(away[p] > 0)
            def _():
                copies[1 + p](c).wait_send()
                copies[3 + p](c).wait_send()

            @pl.when(away[p] == 0)
            def _():
                cross[p](c).wait_send()

            @pl.when(away[p] < line - 1)
            def _():
                copies[6 + p](c).wait_send()
                copies[8 + p](c).wait_send()

    for copy in norms:
        copy.wait()
    whole = slots[0]
    for d in range(1, cols):
        whole = whole + slots[d]
    scale[...] = lax.rsqrt(whole + norm_eps)


def row_reduce(state, grads, step, projected, row_size, col_size, collective_id):
    rows, columns = state.shape
    rank = projected.shape[1]
    chunks = (columns + rank) // WIDTH
    vmem = pl.BlockSpec(memory_space=pltpu.VMEM)
    hbm = pl.BlockSpec(memory_space=pl.ANY)
    size = rank // 8
    f32 = jnp.float32
    operands = (state, projected) if step is None else (state, grads, projected)
    return pl.pallas_call(
        functools.partial(row_kernel, row_size, col_size, step),
        out_shape=[
            jax.ShapeDtypeStruct((rows, rank), f32),
            jax.ShapeDtypeStruct((columns // WIDTH, rank, WIDTH), f32),
            jax.ShapeDtypeStruct((8, rank), f32),
        ],
        in_specs=[hbm] * (len(operands) - 1) + [vmem],
        out_specs=[vmem] * 3,
        scratch_shapes=[
            pltpu.VMEM((chunks, rank, WIDTH), f32),
            pltpu.VMEM((chunks, rank, WIDTH), f32),
            pltpu.VMEM((2, chunks, 3 * size, WIDTH), f32),
            pltpu.VMEM((chunks, 4 * size, WIDTH), f32),
            pltpu.VMEM((2, rank, rows), jnp.bfloat16),
            pltpu.VMEM((rank, rank), f32),
            pltpu.VMEM((32, LANES), f32),
            pltpu.VMEM((rank, LANES), f32),
            pltpu.VMEM((col_size, 8, rank), f32),
            pltpu.VMEM((SLOTS, rows, WIDTH), f32),
        ]
        + ([] if step is None else [pltpu.VMEM((SLOTS, rows, WIDTH), jnp.bfloat16)])
        + [
            pltpu.SemaphoreType.DMA((2, SLOTS)),
            pltpu.SemaphoreType.DMA((KINDS, chunks)),
            pltpu.SemaphoreType.DMA((KINDS, chunks)),
            pltpu.SemaphoreType.DMA((col_size - 1,)),
            pltpu.SemaphoreType.DMA((col_size - 1,)),
        ],
        compiler_params=pltpu.CompilerParams(
            collective_id=collective_id, has_side_effects=True, vmem_limit_bytes=46 * 2**20
        ),
        cost_estimate=pl.CostEstimate(
            flops=6 * rows * columns * rank, bytes_accessed=6 * rows * columns, transcendentals=0
        ),
    )(*operands)


def project_kernel(cols, step, *refs):
    state, grads, right, refs = *refs[:3], refs[3:]
    if step:
        ortho, scale, refs = *refs[:2], refs[2:]
    projected, refs = refs[0], refs[1:]
    if step:
        buffer, refs = refs[0], refs[1:]
    states, slopes, high, low, part, pair, sums, recvs, refs = *refs[:8], refs[8:]
    if step:
        buffers, left, store_sem, refs = *refs[:3], refs[3:]
    load_sem, send_sem, recv_sem = refs
    tall = states.shape[1]
    rows, rank = projected.shape
    columns = state.shape[1]
    blocks = rows // tall
    half = tall // 2
    bits = cols.bit_length() - 1
    me = lax.axis_index("col")
    partners = [me + (1 - 2 * lax.rem(me // (1 << b), 2)) * (1 << b) for b in range(bits)]
    mine = pl.multiple_of(half * lax.rem(me, 2), 8)
    yours = pl.multiple_of(half * (1 - lax.rem(me, 2)), 8)

    def load(r):
        where = pl.ds(r * tall, tall)
        slot = r % 2
        copies = [pltpu.make_async_copy(state.at[where], states.at[slot], load_sem.at[0, slot])]
        for g in range(step + 1):
            copies.append(
                pltpu.make_async_copy(grads.at[g, where], slopes.at[slot, g], load_sem.at[1 + g, slot])
            )
        return copies

    for copy in load(0):
        copy.start()

    barrier = pltpu.get_barrier_semaphore()
    for partner in partners:
        pl.semaphore_signal(barrier, inc=1, device_id={"col": partner}, device_id_type=MESH)

    if step:
        for c in range(columns // WIDTH):
            at = slice(c * WIDTH, (c + 1) * WIDTH)
            high[:, at], low[:, at] = split(right[c])
        left[...] = ortho[...].astype(jnp.bfloat16)
    else:
        high[...], low[...] = split(right[...])

    pl.semaphore_wait(barrier, bits)

    def remote(kind, r, source, target, partner):
        return pltpu.make_async_remote_copy(
            src_ref=source,
            dst_ref=target,
            send_sem=send_sem.at[kind, r],
            recv_sem=recv_sem.at[kind, r],
            device_id={"col": partner},
            device_id_type=MESH,
        )

    def swap(r):
        return remote(0, r, part.at[r, pl.ds(yours, half)], pair.at[r], partners[0])

    def cross(b, r):
        return remote(b, r, sums.at[b - 1, r], recvs.at[b - 1, r], partners[b])

    def whole(r):
        return projected.at[pl.ds(pl.multiple_of(r * tall + mine, 8), half)]

    def gather(r):
        return remote(bits, r, whole(r), whole(r), partners[0])

    def arrive(k, r):
        if k == bits + 1:
            gather(r).wait_recv()
            return
        if k == 1:
            swap(r).wait_recv()
            value = part[r, pl.ds(mine, half), :] + pair[r]
        else:
            cross(k - 1, r).wait_recv()
            value = sums[k - 2, r] + recvs[k - 2, r]
        if k < bits:
            sums[k - 1, r] = value
            cross(k, r).start()
        else:
            if step:
                value = value * scale[0:1, :]
            whole(r)[...] = value
            gather(r).start()

    deep = min(columns, 1024)
    for t in range(blocks + bits + 1):
        if t < blocks:
            slot = t % 2
            if t + 1 < blocks:
                for copy in load(t + 1):
                    copy.start()
            for copy in load(t):
                copy.wait()
            if step and t >= 2:
                store(t - 2).wait()
            part[t] = jnp.zeros(part.shape[1:], jnp.float32)

            @pl.loop(0, columns // deep)
            def _(k):
                at = pl.ds(pl.multiple_of(k * deep, deep), deep)
                value = states[slot, :, at] + slopes[slot, 0, :, at].astype(jnp.float32)
                if step:
                    update = matmul(left[t * tall : (t + 1) * tall, :], high[:, at], ((1,), (0,)), None)
                    value = value - (1.0 - keep_rate) * update
                    value = value + slopes[slot, 1, :, at].astype(jnp.float32)
                    buffers[slot, :, at] = value
                    r_high, r_low, dims = high[:, at], low[:, at], ((1,), (1,))
                else:
                    r_high, r_low, dims = high[at, :], low[at, :], ((1,), (0,))
                v_high, v_low = split(value)
                part[t] += (
                    matmul(v_high, r_high, dims, None)
                    + matmul(v_low, r_high, dims, None)
                    + matmul(v_high, r_low, dims, None)
                )

            if step:
                def store(r):
                    return pltpu.make_async_copy(
                        buffers.at[r % 2], buffer.at[pl.ds(r * tall, tall)], store_sem.at[r % 2]
                    )

                store(t).start()
            swap(t).start()
        for r in range(blocks):
            if 1 <= t - r <= bits + 1:
                arrive(t - r, r)

    for r in range(blocks):
        swap(r).wait_send()
        gather(r).wait_send()
        for b in range(1, bits):
            cross(b, r).wait_send()
        if step and r >= blocks - 2:
            store(r).wait()


def project(state, grads, step, right, ortho, scale, col_size, collective_id):
    rows, columns = state.shape
    rank = right.shape[1]
    tall = min(256, rows)
    blocks = rows // tall
    bits = col_size.bit_length() - 1
    vmem = pl.BlockSpec(memory_space=pltpu.VMEM)
    hbm = pl.BlockSpec(memory_space=pl.ANY)
    f32, bf16 = jnp.float32, jnp.bfloat16
    operands = (state, grads, right) + ((ortho, scale) if step else ())
    shape = (rank, columns) if step else (columns, rank)
    out_shape = [jax.ShapeDtypeStruct((rows, rank), f32)]
    scratch = [
        pltpu.VMEM((2, tall, columns), f32),
        pltpu.VMEM((2, step + 1, tall, columns), bf16),
        pltpu.VMEM(shape, bf16),
        pltpu.VMEM(shape, bf16),
        pltpu.VMEM((blocks, tall, rank), f32),
        pltpu.VMEM((blocks, tall // 2, rank), f32),
        pltpu.VMEM((bits - 1, blocks, tall // 2, rank), f32),
        pltpu.VMEM((bits - 1, blocks, tall // 2, rank), f32),
    ]
    if step:
        out_shape.append(jax.ShapeDtypeStruct((rows, columns), f32))
        scratch += [
            pltpu.VMEM((2, tall, columns), f32),
            pltpu.VMEM((rows, rank), bf16),
            pltpu.SemaphoreType.DMA((2,)),
        ]
    return pl.pallas_call(
        functools.partial(project_kernel, col_size, step),
        out_shape=out_shape,
        in_specs=[hbm, hbm] + [vmem] * (len(operands) - 2),
        out_specs=[vmem, hbm][: step + 1],
        scratch_shapes=scratch
        + [
            pltpu.SemaphoreType.DMA((2 + step, 2)),
            pltpu.SemaphoreType.DMA((bits + 1, blocks)),
            pltpu.SemaphoreType.DMA((bits + 1, blocks)),
        ],
        compiler_params=pltpu.CompilerParams(
            collective_id=collective_id, has_side_effects=True, vmem_limit_bytes=52 * 2**20
        ),
        cost_estimate=pl.CostEstimate(
            flops=8 * rows * columns * rank, bytes_accessed=10 * rows * columns, transcendentals=0
        ),
    )(*operands)


def finish_kernel(gain, buffer, ortho, raw, scale, left, right, before, change, state, lefts, highs):
    @pl.when(pl.program_id(0) == 0)
    def _():
        lefts[0, 0], lefts[0, 1] = split(left[...] * (before[0:1, :] * gain))
        lefts[1, 0], lefts[1, 1] = split(ortho[...] * (scale[0:1, :] * gain))
        highs[...] = ortho[...].astype(jnp.bfloat16)

    dims = ((1,), (0,))
    r_high, r_low = split(raw[0])
    state[...] = buffer[...] - (1.0 - keep_rate) * matmul(highs[...], r_high, dims, None)
    p_high, p_low = split(right[0])
    total = matmul(lefts[0, 0], p_high, dims, None)
    total = total + matmul(lefts[0, 1], p_high, dims, None)
    total = total + matmul(lefts[0, 0], p_low, dims, None)
    total = total + matmul(lefts[1, 0], r_high, dims, None)
    total = total + matmul(lefts[1, 1], r_high, dims, None)
    total = total + matmul(lefts[1, 0], r_low, dims, None)
    change[...] = total.astype(jnp.bfloat16)


def finish(gain, buffer, ortho, raw, scale, left, right, before):
    rows, columns = buffer.shape
    rank = ortho.shape[1]
    tile = pl.BlockSpec((rows, WIDTH), lambda c: (0, c))
    chunk = pl.BlockSpec((1, rank, WIDTH), lambda c: (c, 0, 0))
    tall = pl.BlockSpec((rows, rank), lambda c: (0, 0))
    row = pl.BlockSpec((8, rank), lambda c: (0, 0))
    return pl.pallas_call(
        functools.partial(finish_kernel, gain),
        grid=(columns // WIDTH,),
        out_shape=[
            jax.ShapeDtypeStruct((rows, columns), jnp.bfloat16),
            jax.ShapeDtypeStruct((rows, columns), jnp.float32),
        ],
        in_specs=[tile, tall, chunk, row, tall, chunk, row],
        out_specs=[tile, tile],
        scratch_shapes=[
            pltpu.VMEM((2, 2, rows, rank), jnp.bfloat16),
            pltpu.VMEM((rows, rank), jnp.bfloat16),
        ],
        compiler_params=pltpu.CompilerParams(vmem_limit_bytes=40 * 2**20),
        cost_estimate=pl.CostEstimate(
            flops=14 * rows * columns * rank, bytes_accessed=10 * rows * columns, transcendentals=0
        ),
    )(buffer, ortho, raw, scale, left, right, before)


def shards(row_size, col_size, momentum, grads, basis):
    rank = basis.shape[1]
    gain = (momentum.shape[0] * row_size * momentum.shape[1] * col_size / rank) ** 0.5
    (projected,) = project(momentum, grads, 0, basis, None, None, col_size, 0)
    left, right, before = row_reduce(momentum, grads, 0, projected, row_size, col_size, 1)
    projected, buffer = project(momentum, grads, 1, right, left, before, col_size, 2)
    ortho, raw, scale = row_reduce(buffer, None, None, projected, row_size, col_size, 3)
    return tuple(finish(gain, buffer, ortho, raw, scale, left, right, before))


def solution(mesh):
    return jax.shard_map(
        functools.partial(shards, mesh.shape["row"], mesh.shape["col"]),
        mesh=mesh,
        in_specs=(P("row", "col"), P(None, "row", "col"), P("col", None)),
        out_specs=(P("row", "col"), P("row", "col")),
        check_vma=False,
    )
```

profile of v0, /device:TPU:0, one launch (start us, length us, event | category | flops | bytes accessed | tf_op | source)
XLA Modules:
  0.0 307.8 jit_solution(16498974949618240874)
XLA Ops:
  0.6 28.6 %shard_map.50.refs_2_ = f32[1024,256]{1,0:T(8,128)S(1)} custom-call(f32[1024,4096]{1,0:T(8,128)} %refs_0_.5, bf16[2,1024,4096]{2,1,0:T(8,128)(2,1)} %refs_1_.5, f32[4096,256]{1,0:T(8,128)} %refs_2_.1), custom_call_target="tpu_custom_call" | custom-call | flops 8589934592 | bytes 41943040 | tf_op jit(solution)/shard_map/pallas_call | solution.py:605
  29.2 110.8 %shard_map.51 = (f32[1024,256]{1,0:T(8,128)S(1)}, f32[16,256,256]{2,1,0:T(8,128)S(1)}, f32[8,256]{1,0:T(8,128)S(1)}) custom-call(f32[1024,4096]{1,0:T(8,128)} %refs_0_.5, bf16[2,1024,4096]{2,1,0:T(8,128)(2,1)} %refs_1_.5, f32[1024,256]{1,0:T(8,128)S(1)} %shard_map.50.refs_2_), custom_call_target="tpu_custom_call" | custom-call | flops 6442450944 | bytes 25165824 | tf_op jit(solution)/shard_map/pallas_call | solution.py:395
  140.1 0.0 copy-start
  140.1 2.0 copy-done
  142.1 0.0 copy-start.2
  142.1 1.0 copy-done.2
  143.1 32.8 %shard_map.52 = (f32[1024,256]{1,0:T(8,128)S(1)}, f32[1024,4096]{1,0:T(8,128)}) custom-call(f32[1024,4096]{1,0:T(8,128)} %refs_0_.5, bf16[2,1024,4096]{2,1,0:T(8,128)(2,1)} %refs_1_.5, f32[16,256,256]{2,1,0:T(8,128)} %copy-done, f32[1024,256]{1,0:T(8,128)} %copy-done.2, f32[8,256]{1,0:T(8,128)S(1)} %get-tuple-element.12.refs_4_.before), custom_call_target="tpu_custom_call" | custom-call | flops 8589934592 | bytes 41943040 | tf_op jit(solution)/shard_map/pallas_call | solution.py:605
  175.9 0.0 copy-start.1
  175.9 0.0 copy-start.3
  175.9 108.5 %shard_map.53 = (f32[1024,256]{1,0:T(8,128)S(1)}, f32[16,256,256]{2,1,0:T(8,128)S(1)}, f32[8,256]{1,0:T(8,128)S(1)}) custom-call(f32[1024,4096]{1,0:T(8,128)} %get-tuple-element.13.refs_0_.buffer, f32[1024,256]{1,0:T(8,128)S(1)} %get-tuple-element.14.refs_1_), custom_call_target="tpu_custom_call" | custom-call | flops 6442450944 | bytes 25165824 | tf_op jit(solution)/shard_map/pallas_call | solution.py:395
  284.4 0.0 copy-done.1
  284.4 0.0 copy-done.3
  284.5 23.3 %shard_map.54 = (bf16[1024,4096]{1,0:T(8,128)(2,1)}, f32[1024,4096]{1,0:T(8,128)}) custom-call(f32[1024,4096]{1,0:T(8,128)} %get-tuple-element.13.refs_0_.buffer, f32[1024,256]{1,0:T(8,128)S(1)} %get-tuple-element.15.ortho, f32[16,256,256]{2,1,0:T(8,128)S(1)} %get-tuple-element.16.raw, f32[8,256]{1,0:T(8,128)S(1)} %get-tuple-element.17.scale, ...), custom_call_target="tpu_custom_call" | custom-call | flops 15032385536 | bytes 41943040 | tf_op jit(solution)/shard_map/pallas_call | solution.py:652
Async XLA Ops:
  140.1 2.0 copy-start
  142.1 1.0 copy-start.2
  175.9 108.6 %copy-start.1 = (f32[16,256,256]{2,1,0:T(8,128)S(1)}, f32[16,256,256]{2,1,0:T(8,128)}, u32[]{:S(2)}) copy-start(f32[16,256,256]{2,1,0:T(8,128)} %copy-done) | copy-start | bytes 12582916
  175.9 108.6 %copy-start.3 = (f32[1024,256]{1,0:T(8,128)S(1)}, f32[1024,256]{1,0:T(8,128)}, u32[]{:S(2)}) copy-start(f32[1024,256]{1,0:T(8,128)} %copy-done.2) | copy-start | bytes 3145732
where the time goes:
time: 308 us
  Pallas kernels  304 us (99%)
    pallas_call x2, Pallas kernels, row_reduce(): pl.pallas_call(functools.partial(row_kernel, row_size, col_size, step), o...  219 us
    pallas_call x2, Pallas kernels, project(): pl.pallas_call(functools.partial(project_kernel, col_size, step), out_sha...  61.4 us
    pallas_call x1, Pallas kernels, finish(): pl.pallas_call(functools.partial(finish_kernel, gain), grid=(columns // W...  23.3 us

commit v1 on v0

--- a/solution.py
+++ b/solution.py
@@ -16,6 +16,7 @@
 STRIDE = 2
 SLOTS = 3
 WIDTH = 256
+LAG = 3
 
 
 def matmul(a, b, dims, precision):
@@ -38,7 +39,7 @@
     fin, work, upward, pair, turned, factor, panel, squares, slots, states, refs = *refs[:10], refs[10:]
     if step is not None:
         slopes, refs = refs[0], refs[1:]
-    load_sem, send_sem, recv_sem, norm_send, norm_recv = refs
+    ortho_here, raw_here, load_sem, send_sem, recv_sem, norm_send, norm_recv, out_sem = refs
     line = rows // 2
     rank = factor.shape[0]
     first = rank // WIDTH
@@ -175,7 +176,8 @@
         high, low = split(inverse)
         turned[0, :, :rank] = high
         turned[1, :, :rank] = low
-        ortho[...] = matmul(projected[...], inverse, ((1,), (1,)), HIGHEST)
+        ortho_here[...] = matmul(projected[...], inverse, ((1,), (1,)), HIGHEST)
+        pltpu.make_async_copy(ortho_here, ortho, out_sem.at[chunks - first]).start()
         squares[...] = jnp.zeros_like(squares)
 
     def expand(c):
@@ -183,7 +185,8 @@
         i_high, i_low = turned[0, :, :rank], turned[1, :, :rank]
         dims = ((1,), (0,))
         value = matmul(i_high, t_high, dims, None) + matmul(i_high, t_low, dims, None) + matmul(i_low, t_high, dims, None)
-        raw[c - first] = value
+        raw_here[c - first] = value
+        pltpu.make_async_copy(raw_here.at[c - first], raw.at[c - first], out_sem.at[c - first]).start()
         square = value * value
         squares[...] += sum(square[:, k : k + LANES] for k in range(0, WIDTH, LANES))
 
@@ -374,6 +377,12 @@
             def _():
                 copies[6 + p](c).wait_send()
                 copies[8 + p](c).wait_send()
+
+    pltpu.make_async_copy(ortho_here, ortho, out_sem.at[chunks - first]).wait()
+
+    @pl.loop(0, chunks - first)
+    def _(c):
+        pltpu.make_async_copy(raw_here.at[c], raw.at[c], out_sem.at[c]).wait()
 
     for copy in norms:
         copy.wait()
@@ -400,7 +409,7 @@
             jax.ShapeDtypeStruct((8, rank), f32),
         ],
         in_specs=[hbm] * (len(operands) - 1) + [vmem],
-        out_specs=[vmem] * 3,
+        out_specs=[hbm, hbm, vmem],
         scratch_shapes=[
             pltpu.VMEM((chunks, rank, WIDTH), f32),
             pltpu.VMEM((chunks, rank, WIDTH), f32),
@@ -415,11 +424,14 @@
         ]
         + ([] if step is None else [pltpu.VMEM((SLOTS, rows, WIDTH), jnp.bfloat16)])
         + [
+            pltpu.VMEM((rows, rank), f32),
+            pltpu.VMEM((columns // WIDTH, rank, WIDTH), f32),
             pltpu.SemaphoreType.DMA((2, SLOTS)),
             pltpu.SemaphoreType.DMA((KINDS, chunks)),
             pltpu.SemaphoreType.DMA((KINDS, chunks)),
             pltpu.SemaphoreType.DMA((col_size - 1,)),
             pltpu.SemaphoreType.DMA((col_size - 1,)),
+            pltpu.SemaphoreType.DMA((columns // WIDTH + 1,)),
         ],
         compiler_params=pltpu.CompilerParams(
             collective_id=collective_id, has_side_effects=True, vmem_limit_bytes=46 * 2**20
@@ -439,8 +451,8 @@
         buffer, refs = refs[0], refs[1:]
     states, slopes, high, low, part, pair, sums, recvs, refs = *refs[:8], refs[8:]
     if step:
-        buffers, left, store_sem, refs = *refs[:3], refs[3:]
-    load_sem, send_sem, recv_sem = refs
+        buffers, left, ortho_here, store_sem, refs = *refs[:4], refs[4:]
+    right_here, load_sem, send_sem, recv_sem, right_sem = refs
     tall = states.shape[1]
     rows, rank = projected.shape
     columns = state.shape[1]
@@ -462,20 +474,25 @@
             )
         return copies
 
-    for copy in load(0):
+    fetch = [pltpu.make_async_copy(right, right_here, right_sem.at[0])]
+    if step:
+        fetch.append(pltpu.make_async_copy(ortho, ortho_here, right_sem.at[1]))
+    for copy in fetch + load(0):
         copy.start()
 
     barrier = pltpu.get_barrier_semaphore()
     for partner in partners:
         pl.semaphore_signal(barrier, inc=1, device_id={"col": partner}, device_id_type=MESH)
 
+    for copy in fetch:
+        copy.wait()
     if step:
         for c in range(columns // WIDTH):
             at = slice(c * WIDTH, (c + 1) * WIDTH)
-            high[:, at], low[:, at] = split(right[c])
-        left[...] = ortho[...].astype(jnp.bfloat16)
+            high[:, at], low[:, at] = split(right_here[c])
+        left[...] = ortho_here[...].astype(jnp.bfloat16)
     else:
-        high[...], low[...] = split(right[...])
+        high[...], low[...] = split(right_here[...])
 
     pl.semaphore_wait(barrier, bits)
 
@@ -502,9 +519,6 @@
         return remote(bits, r, whole(r), whole(r), partners[0])
 
     def arrive(k, r):
-        if k == bits + 1:
-            gather(r).wait_recv()
-            return
         if k == 1:
             swap(r).wait_recv()
             value = part[r, pl.ds(mine, half), :] + pair[r]
@@ -520,8 +534,9 @@
             whole(r)[...] = value
             gather(r).start()
 
-    deep = min(columns, 1024)
-    for t in range(blocks + bits + 1):
+    deep = min(columns, 2048)
+    due = {1 + LAG * (k - 1): k for k in range(1, bits + 1)}
+    for t in range(blocks + max(due)):
         if t < blocks:
             slot = t % 2
             if t + 1 < blocks:
@@ -561,12 +576,12 @@
                 store(t).start()
             swap(t).start()
         for r in range(blocks):
-            if 1 <= t - r <= bits + 1:
-                arrive(t - r, r)
+            if t - r in due:
+                arrive(due[t - r], r)
 
     for r in range(blocks):
         swap(r).wait_send()
-        gather(r).wait_send()
+        gather(r).wait()
         for b in range(1, bits):
             cross(b, r).wait_send()
         if step and r >= blocks - 2:
@@ -576,7 +591,7 @@
 def project(state, grads, step, right, ortho, scale, col_size, collective_id):
     rows, columns = state.shape
     rank = right.shape[1]
-    tall = min(256, rows)
+    tall = min(256 if step else 128, rows)
     blocks = rows // tall
     bits = col_size.bit_length() - 1
     vmem = pl.BlockSpec(memory_space=pltpu.VMEM)
@@ -600,18 +615,21 @@
         scratch += [
             pltpu.VMEM((2, tall, columns), f32),
             pltpu.VMEM((rows, rank), bf16),
+            pltpu.VMEM((rows, rank), f32),
             pltpu.SemaphoreType.DMA((2,)),
         ]
     return pl.pallas_call(
         functools.partial(project_kernel, col_size, step),
         out_shape=out_shape,
-        in_specs=[hbm, hbm] + [vmem] * (len(operands) - 2),
+        in_specs=[hbm] * 3 + ([hbm, vmem] if step else []),
         out_specs=[vmem, hbm][: step + 1],
         scratch_shapes=scratch
         + [
+            pltpu.VMEM(right.shape, f32),
             pltpu.SemaphoreType.DMA((2 + step, 2)),
             pltpu.SemaphoreType.DMA((bits + 1, blocks)),
             pltpu.SemaphoreType.DMA((bits + 1, blocks)),
+            pltpu.SemaphoreType.DMA((1 + step,)),
         ],
         compiler_params=pltpu.CompilerParams(
             collective_id=collective_id, has_side_effects=True, vmem_limit_bytes=52 * 2**20
@@ -622,47 +640,69 @@
     )(*operands)
 
 
-def finish_kernel(gain, buffer, ortho, raw, scale, left, right, before, change, state, lefts, highs):
-    @pl.when(pl.program_id(0) == 0)
+def finish_kernel(gain, buffer, ortho, raw, scale, left, right, before, change, state, lefts, highs, news, olds):
+    c = pl.program_id(1)
+    pieces = raw.shape[0]
+
+    @pl.when((pl.program_id(0) == 0) & (c == 0))
     def _():
         lefts[0, 0], lefts[0, 1] = split(left[...] * (before[0:1, :] * gain))
         lefts[1, 0], lefts[1, 1] = split(ortho[...] * (scale[0:1, :] * gain))
         highs[...] = ortho[...].astype(jnp.bfloat16)
 
+    @pl.when(pl.program_id(0) == 0)
+    def _():
+        for k in range(pieces):
+            news[c * pieces + k, 0], news[c * pieces + k, 1] = split(raw[k])
+            olds[c * pieces + k, 0], olds[c * pieces + k, 1] = split(right[k])
+
     dims = ((1,), (0,))
-    r_high, r_low = split(raw[0])
-    state[...] = buffer[...] - (1.0 - keep_rate) * matmul(highs[...], r_high, dims, None)
-    p_high, p_low = split(right[0])
-    total = matmul(lefts[0, 0], p_high, dims, None)
-    total = total + matmul(lefts[0, 1], p_high, dims, None)
-    total = total + matmul(lefts[0, 0], p_low, dims, None)
-    total = total + matmul(lefts[1, 0], r_high, dims, None)
-    total = total + matmul(lefts[1, 1], r_high, dims, None)
-    total = total + matmul(lefts[1, 0], r_low, dims, None)
-    change[...] = total.astype(jnp.bfloat16)
+    tall = buffer.shape[0]
+    here = pl.ds(pl.multiple_of(pl.program_id(0) * tall, tall), tall)
+    for k in range(pieces):
+        at = slice(k * WIDTH, (k + 1) * WIDTH)
+        r_high, r_low = news[c * pieces + k, 0], news[c * pieces + k, 1]
+        p_high, p_low = olds[c * pieces + k, 0], olds[c * pieces + k, 1]
+        state[:, at] = buffer[:, at] - (1.0 - keep_rate) * matmul(highs[here, :], r_high, dims, None)
+        total = matmul(lefts[0, 0, here, :], p_high, dims, None)
+        total = total + matmul(lefts[0, 1, here, :], p_high, dims, None)
+        total = total + matmul(lefts[0, 0, here, :], p_low, dims, None)
+        total = total + matmul(lefts[1, 0, here, :], r_high, dims, None)
+        total = total + matmul(lefts[1, 1, here, :], r_high, dims, None)
+        total = total + matmul(lefts[1, 0, here, :], r_low, dims, None)
+        change[:, at] = total.astype(jnp.bfloat16)
+
+
+TILE_ROWS = 1024
+TILE_PIECES = 2
 
 
 def finish(gain, buffer, ortho, raw, scale, left, right, before):
     rows, columns = buffer.shape
     rank = ortho.shape[1]
-    tile = pl.BlockSpec((rows, WIDTH), lambda c: (0, c))
-    chunk = pl.BlockSpec((1, rank, WIDTH), lambda c: (c, 0, 0))
-    tall = pl.BlockSpec((rows, rank), lambda c: (0, 0))
-    row = pl.BlockSpec((8, rank), lambda c: (0, 0))
+    bf16 = jnp.bfloat16
+    tall, pieces = min(TILE_ROWS, rows), min(TILE_PIECES, columns // WIDTH)
+    tile = pl.BlockSpec((tall, pieces * WIDTH), lambda r, c: (r, c))
+    last = columns // WIDTH // pieces - 1
+    chunk = pl.BlockSpec((pieces, rank, WIDTH), lambda r, c: (jnp.where(r == 0, c, last), 0, 0))
+    whole = pl.BlockSpec((rows, rank), lambda r, c: (0, 0))
+    row = pl.BlockSpec((8, rank), lambda r, c: (0, 0))
     return pl.pallas_call(
         functools.partial(finish_kernel, gain),
-        grid=(columns // WIDTH,),
+        grid=(rows // tall, columns // WIDTH // pieces),
         out_shape=[
-            jax.ShapeDtypeStruct((rows, columns), jnp.bfloat16),
+            jax.ShapeDtypeStruct((rows, columns), bf16),
             jax.ShapeDtypeStruct((rows, columns), jnp.float32),
         ],
-        in_specs=[tile, tall, chunk, row, tall, chunk, row],
+        in_specs=[tile, whole, chunk, row, whole, chunk, row],
         out_specs=[tile, tile],
         scratch_shapes=[
-            pltpu.VMEM((2, 2, rows, rank), jnp.bfloat16),
-            pltpu.VMEM((rows, rank), jnp.bfloat16),
+            pltpu.VMEM((2, 2, rows, rank), bf16),
+            pltpu.VMEM((rows, rank), bf16),
+            pltpu.VMEM((columns // WIDTH, 2, rank, WIDTH), bf16),
+            pltpu.VMEM((columns // WIDTH, 2, rank, WIDTH), bf16),
         ],
-        compiler_params=pltpu.CompilerParams(vmem_limit_bytes=40 * 2**20),
+        compiler_params=pltpu.CompilerParams(vmem_limit_bytes=48 * 2**20),
         cost_estimate=pl.CostEstimate(
             flops=14 * rows * columns * rank, bytes_accessed=10 * rows * columns, transcendentals=0
         ),

time: 308 us -> 299 us (0.971)
  Pallas kernels: 304 us -> 293 us
    pallas_call x2, Pallas kernels: 61.4 us -> 53.3 us  [project(): pl.pallas_call(functools.partial(project_kernel, col_size, step), out_sha...]
where the time goes in v1:
time: 299 us
  Pallas kernels  293 us (98%)
  local copies, waits for them, and re-layouts  4.87 us (2%)
    pallas_call x2, Pallas kernels, row_reduce(): pl.pallas_call(functools.partial(row_kernel, row_size, col_size, step), o...  218 us
    pallas_call x2, Pallas kernels, project(): pl.pallas_call(functools.partial(project_kernel, col_size, step), out_sha...  53.3 us
    pallas_call x1, Pallas kernels, finish(): pl.pallas_call(functools.partial(finish_kernel, gain), grid=(rows // tall...  22.6 us

profile of v1, /device:TPU:0, one launch (start us, length us, event | category | flops | bytes accessed | tf_op | source)
XLA Modules:
  0.0 299.0 jit_solution(14358856528732568316)
XLA Ops:
  0.6 23.9 %shard_map.50.refs_2_ = f32[1024,256]{1,0:T(8,128)S(1)} custom-call(f32[1024,4096]{1,0:T(8,128)} %refs_0_.5, bf16[2,1024,4096]{2,1,0:T(8,128)(2,1)} %refs_1_.5, f32[4096,256]{1,0:T(8,128)} %refs_2_.1), custom_call_target="tpu_custom_call" | custom-call | flops 8589934592 | bytes 41943040 | tf_op jit(solution)/shard_map/pallas_call | solution.py:621
  24.6 108.1 %shard_map.51 = (f32[1024,256]{1,0:T(8,128)S(1)}, f32[16,256,256]{2,1,0:T(8,128)S(1)}, f32[8,256]{1,0:T(8,128)S(1)}) custom-call(f32[1024,4096]{1,0:T(8,128)} %refs_0_.5, bf16[2,1024,4096]{2,1,0:T(8,128)(2,1)} %refs_1_.5, f32[1024,256]{1,0:T(8,128)S(1)} %shard_map.50.refs_2_), custom_call_target="tpu_custom_call" | custom-call | flops 6442450944 | bytes 25165824 | tf_op jit(solution)/shard_map/pallas_call | solution.py:404
  132.7 0.0 copy-start
  132.7 1.9 copy-done
  134.6 0.0 copy-start.1
  134.6 1.0 copy-done.1
  135.6 29.3 %shard_map.52 = (f32[1024,256]{1,0:T(8,128)S(1)}, f32[1024,4096]{1,0:T(8,128)}) custom-call(f32[1024,4096]{1,0:T(8,128)} %refs_0_.5, bf16[2,1024,4096]{2,1,0:T(8,128)(2,1)} %refs_1_.5, f32[16,256,256]{2,1,0:T(8,128)} %copy-done, f32[1024,256]{1,0:T(8,128)} %copy-done.1, f32[8,256]{1,0:T(8,128)S(1)} %get-tuple-element.12.refs_4_.before), custom_call_target="tpu_custom_call" | custom-call | flops 8589934592 | bytes 41943040 | tf_op jit(solution)/shard_map/pallas_call | solution.py:621
  164.9 0.0 copy-start.2
  164.9 109.5 %shard_map.53 = (f32[1024,256]{1,0:T(8,128)S(1)}, f32[16,256,256]{2,1,0:T(8,128)S(1)}, f32[8,256]{1,0:T(8,128)S(1)}) custom-call(f32[1024,4096]{1,0:T(8,128)} %get-tuple-element.13.refs_0_.buffer, f32[1024,256]{1,0:T(8,128)S(1)} %get-tuple-element.14.refs_1_), custom_call_target="tpu_custom_call" | custom-call | flops 6442450944 | bytes 25165824 | tf_op jit(solution)/shard_map/pallas_call | solution.py:404
  274.5 0.0 copy-start.3
  274.5 2.0 copy-done.3
  276.5 0.0 copy-done.2
  276.5 22.6 %shard_map.54 = (bf16[1024,4096]{1,0:T(8,128)(2,1)}, f32[1024,4096]{1,0:T(8,128)}) custom-call(f32[1024,4096]{1,0:T(8,128)} %get-tuple-element.13.refs_0_.buffer, f32[1024,256]{1,0:T(8,128)S(1)} %get-tuple-element.15.ortho, f32[16,256,256]{2,1,0:T(8,128)} %copy-done.3, f32[8,256]{1,0:T(8,128)S(1)} %get-tuple-element.17.scale, f32[1024,256]{1,0:T(8,128)S(1)} %copy-done.2, ...), custom_call_target="tpu_custom_call" | custom-call | flops 15032385536 | bytes 41943040 | tf_op jit(solution)/shard_map/pallas_call | solution.py:690
Async XLA Ops:
  132.7 1.9 copy-start
  134.6 1.0 copy-start.1
  164.9 111.5 %copy-start.2 = (f32[1024,256]{1,0:T(8,128)S(1)}, f32[1024,256]{1,0:T(8,128)}, u32[]{:S(2)}) copy-start(f32[1024,256]{1,0:T(8,128)} %copy-done.1) | copy-start | bytes 3145732
  274.5 2.0 copy-start.3

commit v2 on v1

--- a/solution.py
+++ b/solution.py
@@ -17,6 +17,8 @@
 SLOTS = 3
 WIDTH = 256
 LAG = 3
+SHARE = 40
+EXTRA = 0
 
 
 def matmul(a, b, dims, precision):
@@ -29,6 +31,18 @@
 
 
 KINDS = 12
+
+
+def shares(rank):
+    size = rank * SHARE // 256 // 8 * 8
+    return size, (rank - 4 * size) // 2
+
+
+def inverse_norms(slots, cols):
+    whole = slots[0]
+    for d in range(1, cols):
+        whole = whole + slots[d]
+    return lax.rsqrt(whole + norm_eps)
 
 
 def row_kernel(rows, cols, step, *refs):
@@ -44,7 +58,7 @@
     rank = factor.shape[0]
     first = rank // WIDTH
     chunks = fin.shape[0]
-    size = rank // 8
+    size, wide = shares(rank)
     me = lax.axis_index("row")
     y = lax.rem(me, 2)
     z = me // 2
@@ -55,7 +69,7 @@
     nearer = (me - 2, me + 2)
     farther = (me + 2, me - 2)
     one = tuple(pl.multiple_of(mine + size * p, 8) for p in range(2))
-    two = tuple(4 * size + 2 * size * p for p in range(2))
+    two = tuple(4 * size + wide * p for p in range(2))
 
     def load(j, slot):
         columns = pl.ds(pl.multiple_of(j * WIDTH, WIDTH), WIDTH)
@@ -64,6 +78,17 @@
             copies.append(pltpu.make_async_copy(grads.at[step, :, columns], slopes.at[slot], load_sem.at[1, slot]))
         return copies
 
+    barrier = pltpu.get_barrier_semaphore()
+    pl.semaphore_signal(barrier, inc=1, device_id={"row": partner}, device_id_type=MESH)
+    for p in range(2):
+        @pl.when(away[p] > 0)
+        def _():
+            pl.semaphore_signal(barrier, inc=1, device_id={"row": nearer[p]}, device_id_type=MESH)
+
+    mine_col = lax.axis_index("col")
+    others = [lax.rem(mine_col + d, cols) for d in range(1, cols)] if step is None else []
+    for other in others:
+        pl.semaphore_signal(barrier, inc=1, device_id={"col": other}, device_id_type=MESH)
     for j in range(SLOTS - 1):
         for copy in load(j, j):
             copy.start()
@@ -84,16 +109,16 @@
         up = upward.at[p]
         copies[1 + p] = functools.partial(send, 1 + p, source=work, start=o, target=up, at=0, count=size, device=n)
         copies[3 + p] = functools.partial(
-            send, 3 + p, source=work, start=t, target=up, at=size, count=2 * size, device=n
+            send, 3 + p, source=work, start=t, target=up, at=size, count=wide, device=n
         )
         copies[6 + p] = functools.partial(send, 6 + p, source=fin, start=o, target=fin, at=o, count=size, device=f)
-        copies[8 + p] = functools.partial(send, 8 + p, source=fin, start=t, target=fin, at=t, count=2 * size, device=f)
+        copies[8 + p] = functools.partial(send, 8 + p, source=fin, start=t, target=fin, at=t, count=wide, device=f)
         copies[10 + p] = functools.partial(
             send, 10 + p, source=fin, start=o, target=fin, at=o, count=size, device=partner
         )
     cross = [
         functools.partial(
-            send, 5, source=work, start=two[p], target=pair, at=2 * size, count=2 * size, device=partner
+            send, 5, source=work, start=two[p], target=pair, at=2 * size, count=wide, device=partner
         )
         for p in range(2)
     ]
@@ -109,21 +134,10 @@
     for k in range(first):
         work[k] = gram[:, k * WIDTH : (k + 1) * WIDTH]
 
-    barrier = pltpu.get_barrier_semaphore()
-    pl.semaphore_signal(barrier, inc=1, device_id={"row": partner}, device_id_type=MESH)
-    for p in range(2):
-        @pl.when(away[p] > 0)
-        def _():
-            pl.semaphore_signal(barrier, inc=1, device_id={"row": nearer[p]}, device_id_type=MESH)
-
-    mine_col = lax.axis_index("col")
-    others = [lax.rem(mine_col + d, cols) for d in range(1, cols)]
-    for other in others:
-        pl.semaphore_signal(barrier, inc=1, device_id={"col": other}, device_id_type=MESH)
-    pl.semaphore_wait(barrier, jnp.where((z == 0) | (z == line - 1), 2, 3) + cols - 1)
+    pl.semaphore_wait(barrier, jnp.where((z == 0) | (z == line - 1), 2, 3) + len(others))
 
     turn = line * STRIDE
-    delay = max(turn, chunks + 1 - 2 * STRIDE) - turn
+    delay = max(turn, chunks + 1 - 2 * STRIDE + EXTRA) - turn
     last = 2 * turn + delay
 
     block = 32
@@ -261,7 +275,7 @@
             @pl.when(away[p] < line - 1)
             def _():
                 copies[3 + p](c).wait_recv()
-                add(work, c, two[p], upward.at[p], size, 2 * size)
+                add(work, c, two[p], upward.at[p], size, wide)
 
             @pl.when(away[p] > 0)
             def _():
@@ -272,7 +286,7 @@
 
         def crossed(c, p):
             cross[p](c).wait_recv()
-            add(fin, c, two[p], pair, 2 * size, 2 * size)
+            add(fin, c, two[p], pair, 2 * size, wide)
 
         def fall(c, p):
             @pl.when(away[p] > 0)
@@ -344,7 +358,11 @@
     def _(c):
         expand(c)
 
-    slots[mine_col] = matmul(jnp.ones((8, LANES), jnp.float32), squares[...], ((1,), (1,)), HIGHEST)
+    own = matmul(jnp.ones((8, LANES), jnp.float32), squares[...], ((1,), (1,)), HIGHEST)
+    if step is None:
+        slots[mine_col] = own
+    else:
+        scale[...] = own
     norms = [
         pltpu.make_async_remote_copy(
             src_ref=slots.at[mine_col],
@@ -384,12 +402,10 @@
     def _(c):
         pltpu.make_async_copy(raw_here.at[c], raw.at[c], out_sem.at[c]).wait()
 
-    for copy in norms:
-        copy.wait()
-    whole = slots[0]
-    for d in range(1, cols):
-        whole = whole + slots[d]
-    scale[...] = lax.rsqrt(whole + norm_eps)
+    if step is None:
+        for copy in norms:
+            copy.wait()
+        scale[...] = inverse_norms(slots, cols)
 
 
 def row_reduce(state, grads, step, projected, row_size, col_size, collective_id):
@@ -397,8 +413,8 @@
     rank = projected.shape[1]
     chunks = (columns + rank) // WIDTH
     vmem = pl.BlockSpec(memory_space=pltpu.VMEM)
-    hbm = pl.BlockSpec(memory_space=pl.ANY)
-    size = rank // 8
+    hbm = pl.BlockSpec(memory_space=pltpu.HBM)
+    size, wide = shares(rank)
     f32 = jnp.float32
     operands = (state, projected) if step is None else (state, grads, projected)
     return pl.pallas_call(
@@ -413,8 +429,8 @@
         scratch_shapes=[
             pltpu.VMEM((chunks, rank, WIDTH), f32),
             pltpu.VMEM((chunks, rank, WIDTH), f32),
-            pltpu.VMEM((2, chunks, 3 * size, WIDTH), f32),
-            pltpu.VMEM((chunks, 4 * size, WIDTH), f32),
+            pltpu.VMEM((2, chunks, size + wide, WIDTH), f32),
+            pltpu.VMEM((chunks, 2 * size + wide, WIDTH), f32),
             pltpu.VMEM((2, rank, rows), jnp.bfloat16),
             pltpu.VMEM((rank, rank), f32),
             pltpu.VMEM((32, LANES), f32),
@@ -434,7 +450,7 @@
             pltpu.SemaphoreType.DMA((columns // WIDTH + 1,)),
         ],
         compiler_params=pltpu.CompilerParams(
-            collective_id=collective_id, has_side_effects=True, vmem_limit_bytes=46 * 2**20
+            collective_id=collective_id, has_side_effects=True, vmem_limit_bytes=62 * 2**20
         ),
         cost_estimate=pl.CostEstimate(
             flops=6 * rows * columns * rank, bytes_accessed=6 * rows * columns, transcendentals=0
@@ -445,13 +461,13 @@
 def project_kernel(cols, step, *refs):
     state, grads, right, refs = *refs[:3], refs[3:]
     if step:
-        ortho, scale, refs = *refs[:2], refs[2:]
+        ortho, norms, refs = *refs[:2], refs[2:]
     projected, refs = refs[0], refs[1:]
     if step:
-        buffer, refs = refs[0], refs[1:]
+        buffer, scale, refs = *refs[:2], refs[2:]
     states, slopes, high, low, part, pair, sums, recvs, refs = *refs[:8], refs[8:]
     if step:
-        buffers, left, ortho_here, store_sem, refs = *refs[:4], refs[4:]
+        buffers, left, ortho_here, slots, store_sem, norm_send, norm_recv, refs = *refs[:7], refs[7:]
     right_here, load_sem, send_sem, recv_sem, right_sem = refs
     tall = states.shape[1]
     rows, rank = projected.shape
@@ -481,8 +497,9 @@
         copy.start()
 
     barrier = pltpu.get_barrier_semaphore()
-    for partner in partners:
-        pl.semaphore_signal(barrier, inc=1, device_id={"col": partner}, device_id_type=MESH)
+    others = [lax.rem(me + d, cols) for d in range(1, cols)] if step else []
+    for other in others if step else partners:
+        pl.semaphore_signal(barrier, inc=1, device_id={"col": other}, device_id_type=MESH)
 
     for copy in fetch:
         copy.wait()
@@ -494,7 +511,22 @@
     else:
         high[...], low[...] = split(right_here[...])
 
-    pl.semaphore_wait(barrier, bits)
+    pl.semaphore_wait(barrier, len(others) if step else bits)
+    exchange = [
+        pltpu.make_async_remote_copy(
+            src_ref=norms,
+            dst_ref=slots.at[me],
+            send_sem=norm_send.at[d],
+            recv_sem=norm_recv.at[d],
+            device_id={"col": other},
+            device_id_type=MESH,
+        )
+        for d, other in enumerate(others)
+    ]
+    for copy in exchange:
+        copy.start()
+    if step:
+        slots[me] = norms[...]
 
     def remote(kind, r, source, target, partner):
         return pltpu.make_async_remote_copy(
@@ -575,6 +607,10 @@
 
                 store(t).start()
             swap(t).start()
+            if step and t == 0:
+                for copy in exchange:
+                    copy.wait()
+                scale[...] = inverse_norms(slots, cols)
         for r in range(blocks):
             if t - r in due:
                 arrive(due[t - r], r)
@@ -588,16 +624,16 @@
             store(r).wait()
 
 
-def project(state, grads, step, right, ortho, scale, col_size, collective_id):
+def project(state, grads, step, right, ortho, norms, col_size, collective_id):
     rows, columns = state.shape
     rank = right.shape[1]
     tall = min(256 if step else 128, rows)
     blocks = rows // tall
     bits = col_size.bit_length() - 1
     vmem = pl.BlockSpec(memory_space=pltpu.VMEM)
-    hbm = pl.BlockSpec(memory_space=pl.ANY)
+    hbm = pl.BlockSpec(memory_space=pltpu.HBM)
     f32, bf16 = jnp.float32, jnp.bfloat16
-    operands = (state, grads, right) + ((ortho, scale) if step else ())
+    operands = (state, grads, right) + ((ortho, norms) if step else ())
     shape = (rank, columns) if step else (columns, rank)
     out_shape = [jax.ShapeDtypeStruct((rows, rank), f32)]
     scratch = [
@@ -611,18 +647,21 @@
         pltpu.VMEM((bits - 1, blocks, tall // 2, rank), f32),
     ]
     if step:
-        out_shape.append(jax.ShapeDtypeStruct((rows, columns), f32))
+        out_shape += [jax.ShapeDtypeStruct((rows, columns), f32), jax.ShapeDtypeStruct((8, rank), f32)]
         scratch += [
             pltpu.VMEM((2, tall, columns), f32),
             pltpu.VMEM((rows, rank), bf16),
             pltpu.VMEM((rows, rank), f32),
+            pltpu.VMEM((col_size, 8, rank), f32),
             pltpu.SemaphoreType.DMA((2,)),
+            pltpu.SemaphoreType.DMA((col_size - 1,)),
+            pltpu.SemaphoreType.DMA((col_size - 1,)),
         ]
     return pl.pallas_call(
         functools.partial(project_kernel, col_size, step),
         out_shape=out_shape,
         in_specs=[hbm] * 3 + ([hbm, vmem] if step else []),
-        out_specs=[vmem, hbm][: step + 1],
+        out_specs=[vmem, hbm, vmem] if step else [vmem],
         scratch_shapes=scratch
         + [
             pltpu.VMEM(right.shape, f32),
@@ -632,7 +671,7 @@
             pltpu.SemaphoreType.DMA((1 + step,)),
         ],
         compiler_params=pltpu.CompilerParams(
-            collective_id=collective_id, has_side_effects=True, vmem_limit_bytes=52 * 2**20
+            collective_id=collective_id, has_side_effects=True, vmem_limit_bytes=62 * 2**20
         ),
         cost_estimate=pl.CostEstimate(
             flops=8 * rows * columns * rank, bytes_accessed=10 * rows * columns, transcendentals=0
@@ -713,8 +752,8 @@
     rank = basis.shape[1]
     gain = (momentum.shape[0] * row_size * momentum.shape[1] * col_size / rank) ** 0.5
     (projected,) = project(momentum, grads, 0, basis, None, None, col_size, 0)
-    left, right, before = row_reduce(momentum, grads, 0, projected, row_size, col_size, 1)
-    projected, buffer = project(momentum, grads, 1, right, left, before, col_size, 2)
+    left, right, norms = row_reduce(momentum, grads, 0, projected, row_size, col_size, 1)
+    projected, buffer, before = project(momentum, grads, 1, right, left, norms, col_size, 2)
     ortho, raw, scale = row_reduce(buffer, None, None, projected, row_size, col_size, 3)
     return tuple(finish(gain, buffer, ortho, raw, scale, left, right, before))
 

time: 299 us -> 294 us (0.983)
    pallas_call x2, Pallas kernels: 218 us -> 215 us  [row_reduce(): pl.pallas_call(functools.partial(row_kernel, row_size, col_size, step), o...]
where the time goes in v2:
time: 294 us; the launch traced here: 293 us
  Pallas kernels  291 us (99%)
    pallas_call x2, Pallas kernels, row_reduce(): pl.pallas_call(functools.partial(row_kernel, row_size, col_size, step), o...  215 us
    pallas_call x2, Pallas kernels, project(): pl.pallas_call(functools.partial(project_kernel, col_size, step), out_sha...  53.7 us
    pallas_call x1, Pallas kernels, finish(): pl.pallas_call(functools.partial(finish_kernel, gain), grid=(rows // tall...  22.6 us

profile of v2, /device:TPU:0, one launch (start us, length us, event | category | flops | bytes accessed | tf_op | source)
XLA Modules:
  0.0 293.5 jit_solution(1466471463962599879)
XLA Ops:
  0.6 24.9 %shard_map.50.refs_2_ = f32[1024,256]{1,0:T(8,128)} custom-call(f32[1024,4096]{1,0:T(8,128)} %refs_0_.5, bf16[2,1024,4096]{2,1,0:T(8,128)(2,1)} %refs_1_.5, f32[4096,256]{1,0:T(8,128)} %refs_2_.1), custom_call_target="tpu_custom_call" | custom-call | flops 8589934592 | bytes 41943040 | tf_op jit(solution)/shard_map/pallas_call | solution.py:660
  25.6 106.4 %shard_map.51 = (f32[1024,256]{1,0:T(8,128)}, f32[16,256,256]{2,1,0:T(8,128)}, f32[8,256]{1,0:T(8,128)}) custom-call(f32[1024,4096]{1,0:T(8,128)} %refs_0_.5, bf16[2,1024,4096]{2,1,0:T(8,128)(2,1)} %refs_1_.5, f32[1024,256]{1,0:T(8,128)} %shard_map.50.refs_2_), custom_call_target="tpu_custom_call" | custom-call | flops 6442450944 | bytes 25165824 | tf_op jit(solution)/shard_map/pallas_call | solution.py:420
  131.9 28.8 %shard_map.52 = (f32[1024,256]{1,0:T(8,128)}, f32[1024,4096]{1,0:T(8,128)}, f32[8,256]{1,0:T(8,128)}) custom-call(f32[1024,4096]{1,0:T(8,128)} %refs_0_.5, bf16[2,1024,4096]{2,1,0:T(8,128)(2,1)} %refs_1_.5, f32[16,256,256]{2,1,0:T(8,128)} %get-tuple-element.11.refs_2_.right, f32[1024,256]{1,0:T(8,128)} %get-tuple-element.12.refs_3_.left, ...), custom_call_target="tpu_custom_call" | custom-call | flops 8589934592 | bytes 41943040 | tf_op jit(solution)/shard_map/pallas_call | solution.py:660
  160.7 0.0 copy-start
  160.7 0.0 copy-start.1
  160.7 108.2 %shard_map.53 = (f32[1024,256]{1,0:T(8,128)}, f32[16,256,256]{2,1,0:T(8,128)}, f32[8,256]{1,0:T(8,128)}) custom-call(f32[1024,4096]{1,0:T(8,128)} %get-tuple-element.14.refs_0_.buffer, f32[1024,256]{1,0:T(8,128)} %get-tuple-element.15.refs_1_), custom_call_target="tpu_custom_call" | custom-call | flops 6442450944 | bytes 25165824 | tf_op jit(solution)/shard_map/pallas_call | solution.py:420
  269.0 0.0 copy-done
  269.0 0.0 copy-done.1
  269.0 0.0 copy-start.2
  269.0 1.2 copy-done.2
  270.2 0.0 copy-start.3
  270.2 0.7 copy-done.3
  270.9 22.6 %shard_map.54 = (bf16[1024,4096]{1,0:T(8,128)(2,1)}, f32[1024,4096]{1,0:T(8,128)}) custom-call(f32[1024,4096]{1,0:T(8,128)} %get-tuple-element.14.refs_0_.buffer, f32[1024,256]{1,0:T(8,128)S(1)} %copy-done.2, f32[16,256,256]{2,1,0:T(8,128)} %get-tuple-element.17.raw, f32[8,256]{1,0:T(8,128)S(1)} %copy-done.3, f32[1024,256]{1,0:T(8,128)S(1)} %copy-done, ...), custom_call_target="tpu_custom_call" | custom-call | flops 15032385536 | bytes 41943040 | tf_op jit(solution)/shard_map/pallas_call | solution.py:729
Async XLA Ops:
  160.7 108.2 %copy-start = (f32[1024,256]{1,0:T(8,128)S(1)}, f32[1024,256]{1,0:T(8,128)}, u32[]{:S(2)}) copy-start(f32[1024,256]{1,0:T(8,128)} %get-tuple-element.12.refs_3_.left) | copy-start | bytes 3145732
  160.7 108.2 %copy-start.1 = (f32[8,256]{1,0:T(8,128)S(1)}, f32[8,256]{1,0:T(8,128)}, u32[]{:S(2)}) copy-start(f32[8,256]{1,0:T(8,128)} %get-tuple-element.19.before) | copy-start | bytes 24580
  269.0 1.2 copy-start.2
  270.2 0.7 copy-start.3

commit v3 on v2

--- a/solution.py
+++ b/solution.py
@@ -18,7 +18,7 @@
 WIDTH = 256
 LAG = 3
 SHARE = 40
-EXTRA = 0
+EXTRA = 1
 
 
 def matmul(a, b, dims, precision):
@@ -741,7 +741,7 @@
             pltpu.VMEM((columns // WIDTH, 2, rank, WIDTH), bf16),
             pltpu.VMEM((columns // WIDTH, 2, rank, WIDTH), bf16),
         ],
-        compiler_params=pltpu.CompilerParams(vmem_limit_bytes=48 * 2**20),
+        compiler_params=pltpu.CompilerParams(vmem_limit_bytes=62 * 2**20),
         cost_estimate=pl.CostEstimate(
             flops=14 * rows * columns * rank, bytes_accessed=10 * rows * columns, transcendentals=0
         ),

time: 294 us -> 289 us (0.983)
  Pallas kernels: 291 us -> 288 us
    pallas_call x2, Pallas kernels: 215 us -> 211 us  [row_reduce(): pl.pallas_call(functools.partial(row_kernel, row_size, col_size, step), o...]
where the time goes in v3:
time: 289 us
  Pallas kernels  288 us (100%)
    pallas_call x2, Pallas kernels, row_reduce(): pl.pallas_call(functools.partial(row_kernel, row_size, col_size, step), o...  211 us
    pallas_call x2, Pallas kernels, project(): pl.pallas_call(functools.partial(project_kernel, col_size, step), out_sha...  53.7 us
    pallas_call x1, Pallas kernels, finish(): pl.pallas_call(functools.partial(finish_kernel, gain), grid=(rows // tall...  23.5 us

profile of v3, /device:TPU:0, one launch (start us, length us, event | category | flops | bytes accessed | tf_op | source)
XLA Modules:
  0.0 289.0 jit_solution(10611672015207337677)
XLA Ops:
  0.6 24.9 %shard_map.50.refs_2_ = f32[1024,256]{1,0:T(8,128)} custom-call(f32[1024,4096]{1,0:T(8,128)} %refs_0_.5, bf16[2,1024,4096]{2,1,0:T(8,128)(2,1)} %refs_1_.5, f32[4096,256]{1,0:T(8,128)} %refs_2_.1), custom_call_target="tpu_custom_call" | custom-call | flops 8589934592 | bytes 41943040 | tf_op jit(solution)/shard_map/pallas_call | solution.py:660
  25.6 104.4 %shard_map.51 = (f32[1024,256]{1,0:T(8,128)}, f32[16,256,256]{2,1,0:T(8,128)}, f32[8,256]{1,0:T(8,128)}) custom-call(f32[1024,4096]{1,0:T(8,128)} %refs_0_.5, bf16[2,1024,4096]{2,1,0:T(8,128)(2,1)} %refs_1_.5, f32[1024,256]{1,0:T(8,128)} %shard_map.50.refs_2_), custom_call_target="tpu_custom_call" | custom-call | flops 6442450944 | bytes 25165824 | tf_op jit(solution)/shard_map/pallas_call | solution.py:420
  130.0 28.8 %shard_map.52 = (f32[1024,256]{1,0:T(8,128)}, f32[1024,4096]{1,0:T(8,128)}, f32[8,256]{1,0:T(8,128)}) custom-call(f32[1024,4096]{1,0:T(8,128)} %refs_0_.5, bf16[2,1024,4096]{2,1,0:T(8,128)(2,1)} %refs_1_.5, f32[16,256,256]{2,1,0:T(8,128)} %get-tuple-element.11.refs_2_.right, f32[1024,256]{1,0:T(8,128)} %get-tuple-element.12.refs_3_.left, ...), custom_call_target="tpu_custom_call" | custom-call | flops 8589934592 | bytes 41943040 | tf_op jit(solution)/shard_map/pallas_call | solution.py:660
  158.8 106.8 %shard_map.53 = (f32[1024,256]{1,0:T(8,128)}, f32[16,256,256]{2,1,0:T(8,128)}, f32[8,256]{1,0:T(8,128)}) custom-call(f32[1024,4096]{1,0:T(8,128)} %get-tuple-element.14.refs_0_.buffer, f32[1024,256]{1,0:T(8,128)} %get-tuple-element.15.refs_1_), custom_call_target="tpu_custom_call" | custom-call | flops 6442450944 | bytes 25165824 | tf_op jit(solution)/shard_map/pallas_call | solution.py:420
  265.6 23.5 %shard_map.54 = (bf16[1024,4096]{1,0:T(8,128)(2,1)}, f32[1024,4096]{1,0:T(8,128)}) custom-call(f32[1024,4096]{1,0:T(8,128)} %get-tuple-element.14.refs_0_.buffer, f32[1024,256]{1,0:T(8,128)} %get-tuple-element.16.ortho, f32[16,256,256]{2,1,0:T(8,128)} %get-tuple-element.17.raw, f32[8,256]{1,0:T(8,128)} %get-tuple-element.18.scale, ...), custom_call_target="tpu_custom_call" | custom-call | flops 15032385536 | bytes 41943040 | tf_op jit(solution)/shard_map/pallas_call | solution.py:729

commit v4 on v3

--- a/solution.py
+++ b/solution.py
@@ -493,7 +493,7 @@
     fetch = [pltpu.make_async_copy(right, right_here, right_sem.at[0])]
     if step:
         fetch.append(pltpu.make_async_copy(ortho, ortho_here, right_sem.at[1]))
-    for copy in fetch + load(0):
+    for copy in fetch + load(0) + (load(1) if blocks > 1 else []):
         copy.start()
 
     barrier = pltpu.get_barrier_semaphore()
@@ -571,7 +571,7 @@
     for t in range(blocks + max(due)):
         if t < blocks:
             slot = t % 2
-            if t + 1 < blocks:
+            if 1 <= t < blocks - 1:
                 for copy in load(t + 1):
                     copy.start()
             for copy in load(t):

time: 289 us -> 293 us (1.014)
  Pallas kernels: 288 us -> 292 us
    pallas_call x2, Pallas kernels: 53.7 us -> 57.1 us  [project(): pl.pallas_call(functools.partial(project_kernel, col_size, step), out_sha...]
where the time goes in v4:
time: 293 us; the launch traced here: 292 us
  Pallas kernels  292 us (100%)
    pallas_call x2, Pallas kernels, row_reduce(): pl.pallas_call(functools.partial(row_kernel, row_size, col_size, step), o...  211 us
    pallas_call x2, Pallas kernels, project(): pl.pallas_call(functools.partial(project_kernel, col_size, step), out_sha...  57.1 us
    pallas_call x1, Pallas kernels, finish(): pl.pallas_call(functools.partial(finish_kernel, gain), grid=(rows // tall...  23.5 us

profile of v4, /device:TPU:0, one launch (start us, length us, event | category | flops | bytes accessed | tf_op | source)
XLA Modules:
  0.0 292.3 jit_solution(17207050660131864580)
XLA Ops:
  0.6 25.4 %shard_map.50.refs_2_ = f32[1024,256]{1,0:T(8,128)} custom-call(f32[1024,4096]{1,0:T(8,128)} %refs_0_.5, bf16[2,1024,4096]{2,1,0:T(8,128)(2,1)} %refs_1_.5, f32[4096,256]{1,0:T(8,128)} %refs_2_.1), custom_call_target="tpu_custom_call" | custom-call | flops 8589934592 | bytes 41943040 | tf_op jit(solution)/shard_map/pallas_call | solution.py:660
  26.1 104.4 %shard_map.51 = (f32[1024,256]{1,0:T(8,128)}, f32[16,256,256]{2,1,0:T(8,128)}, f32[8,256]{1,0:T(8,128)}) custom-call(f32[1024,4096]{1,0:T(8,128)} %refs_0_.5, bf16[2,1024,4096]{2,1,0:T(8,128)(2,1)} %refs_1_.5, f32[1024,256]{1,0:T(8,128)} %shard_map.50.refs_2_), custom_call_target="tpu_custom_call" | custom-call | flops 6442450944 | bytes 25165824 | tf_op jit(solution)/shard_map/pallas_call | solution.py:420
  130.5 31.7 %shard_map.52 = (f32[1024,256]{1,0:T(8,128)}, f32[1024,4096]{1,0:T(8,128)}, f32[8,256]{1,0:T(8,128)}) custom-call(f32[1024,4096]{1,0:T(8,128)} %refs_0_.5, bf16[2,1024,4096]{2,1,0:T(8,128)(2,1)} %refs_1_.5, f32[16,256,256]{2,1,0:T(8,128)} %get-tuple-element.11.refs_2_.right, f32[1024,256]{1,0:T(8,128)} %get-tuple-element.12.refs_3_.left, ...), custom_call_target="tpu_custom_call" | custom-call | flops 8589934592 | bytes 41943040 | tf_op jit(solution)/shard_map/pallas_call | solution.py:660
  162.1 106.7 %shard_map.53 = (f32[1024,256]{1,0:T(8,128)}, f32[16,256,256]{2,1,0:T(8,128)}, f32[8,256]{1,0:T(8,128)}) custom-call(f32[1024,4096]{1,0:T(8,128)} %get-tuple-element.14.refs_0_.buffer, f32[1024,256]{1,0:T(8,128)} %get-tuple-element.15.refs_1_), custom_call_target="tpu_custom_call" | custom-call | flops 6442450944 | bytes 25165824 | tf_op jit(solution)/shard_map/pallas_call | solution.py:420
  268.8 23.5 %shard_map.54 = (bf16[1024,4096]{1,0:T(8,128)(2,1)}, f32[1024,4096]{1,0:T(8,128)}) custom-call(f32[1024,4096]{1,0:T(8,128)} %get-tuple-element.14.refs_0_.buffer, f32[1024,256]{1,0:T(8,128)} %get-tuple-element.16.ortho, f32[16,256,256]{2,1,0:T(8,128)} %get-tuple-element.17.raw, f32[8,256]{1,0:T(8,128)} %get-tuple-element.18.scale, ...), custom_call_target="tpu_custom_call" | custom-call | flops 15032385536 | bytes 41943040 | tf_op jit(solution)/shard_map/pallas_call | solution.py:729
